TPU v7x, 32 devices: a whole 2x2x4 slice. The times are simulated.
32 devices in a mesh: replica: 8 (over z, y), tp: 4 (over x, core).
Axes of the slice: x: 2, y: 2, z: 4, core: 2. Of those that a mesh axis runs over, the one named last changes fastest.
Arguments:
- hidden: bfloat16 [96, 4, 8192], P('replica', None, 'tp'), may hold values from -6 to 6
- norm_gain: float32 [8192], replicated, may hold values from 0.5 to 1.5
- w_query: float32 [8192, 4096], P(('replica', 'tp')), may hold values from -0.0625 to 0.0625
- w_key: float32 [8192, 512], P(('replica', 'tp')), may hold values from -0.0625 to 0.0625
- w_value: float32 [8192, 512], P(('replica', 'tp')), may hold values from -0.0625 to 0.0625
- bias_query: float32 [4096], P('tp'), may hold values from -3 to 3
- bias_key: float32 [512], P('tp'), may hold values from -3 to 3
- bias_value: float32 [512], P('tp'), may hold values from -3 to 3
- key_pages: bfloat16 [512, 4, 128, 128], P(('replica', 'tp')), may hold values from -256 to 256
- value_pages: bfloat16 [512, 4, 128, 128], P(('replica', 'tp')), may hold values from -6 to 6
- kv_lengths: int32 [96], P(('replica', 'tp')), may hold values from 1 to 1024, as said below
- page_table: int32 [96, 8], P(('replica', 'tp')), may hold values from 0 to 15, as said below
Outputs:
- attended: bfloat16 [96, 4, 4096], P(('replica', 'tp'))
Inputs may be any that keep to these rules, and one draw needn't show every extreme that they name: `kv_lengths`: on every device, one row has exactly 1024 cached tokens. `page_table`: page ids are local to the pool of 16 pages of the device that holds the row. The first ceil(kv_lengths / 128) entries of a row name its pages in order; no page serves two of those entries on one device; later entries are arbitrary pages of the pool.
All inputs are finite; a program needn't handle non-finite values.
Results may differ from a plain program's by a relative error of at most 0.04.
Values may be sent and summed in bfloat16 or wider, within the bound.
No kernel may reach another device: no remote copies, remote signals or barrier semaphores. Data moves between devices by JAX's collectives and lax.ppermute only.
A program may use at most 128 MiB of HBM per device.

v0:
```python
import jax
import jax.numpy as jnp
from jax import lax
from jax.sharding import PartitionSpec as P

HD = 128
HQ = 32
KVH = 4
PAGE = 128
MOSTP = 8
EPS = 1e-06
THETA = 1000000.0


def rotate(values, positions):
    half = values.shape[-1] // 2
    freq = THETA ** (-(jnp.arange(half, dtype=jnp.float32) * 2.0 / values.shape[-1]))
    angle = positions.astype(jnp.float32)[..., None] * freq
    angle = jnp.concatenate([angle, angle], -1)[:, :, None, :]
    turned = jnp.concatenate([-values[..., half:], values[..., :half]], -1)
    return values * jnp.cos(angle) + turned * jnp.sin(angle)


def on_device(
    hidden,
    norm_gain,
    w_query,
    w_key,
    w_value,
    bias_query,
    bias_key,
    bias_value,
    key_pages,
    value_pages,
    kv_lengths,
    page_table,
):
    shards = (
        w_query.astype(jnp.bfloat16),
        w_key.astype(jnp.bfloat16),
        w_value.astype(jnp.bfloat16),
    )
    whole = lax.all_gather(hidden, "tp", axis=2, tiled=True)
    count, steps, width = whole.shape
    wide = whole.astype(jnp.float32)
    power = jnp.mean(wide * wide, axis=2, keepdims=True)
    normed = (
        (wide * lax.rsqrt(power + EPS) * norm_gain)
        .astype(jnp.bfloat16)
        .reshape(count * steps, width)
    )
    local = (
        lax.all_to_all(shards[0], "tp", split_axis=1, concat_axis=0, tiled=True),
        lax.all_to_all(shards[1], "tp", split_axis=1, concat_axis=0, tiled=True),
        lax.all_to_all(shards[2], "tp", split_axis=1, concat_axis=0, tiled=True),
    )
    pieces = (
        lax.all_gather(local[0], "replica", axis=0, tiled=True),
        lax.all_gather(local[1], "replica", axis=0, tiled=True),
        lax.all_gather(local[2], "replica", axis=0, tiled=True),
    )
    sums = tuple((jnp.dot(normed, piece, preferred_element_type=jnp.float32) for piece in pieces))
    made = [
        (total + bias).astype(jnp.bfloat16).reshape(count, steps, -1)
        for total, bias in zip(sums, (bias_query, bias_key, bias_value))
    ]
    query, key_new, value_new = (
        lax.all_to_all(made[0], "tp", split_axis=0, concat_axis=2, tiled=True),
        lax.all_to_all(made[1], "tp", split_axis=0, concat_axis=2, tiled=True),
        lax.all_to_all(made[2], "tp", split_axis=0, concat_axis=2, tiled=True),
    )
    rows = query.shape[0]
    steps = query.shape[1]
    query = query.reshape(rows, steps, HQ, HD)
    key_new = key_new.reshape(rows, steps, KVH, HD)
    value_new = value_new.reshape(rows, steps, KVH, HD)
    positions = kv_lengths[:, None] + jnp.arange(steps, dtype=jnp.int32)[None, :]
    query_rot = rotate(query.astype(jnp.float32), positions).astype(jnp.bfloat16)
    key_rot = rotate(key_new.astype(jnp.float32), positions).astype(jnp.bfloat16)
    group = HQ // KVH
    scale = 1.0 / HD**0.5
    q_heads = query_rot.reshape(rows, steps, KVH, group, HD)
    keys = jnp.take(key_pages, page_table, axis=0)
    vals = jnp.take(value_pages, page_table, axis=0)
    cache = (
        jnp.einsum("rtkgd,rmknd->rtkgmn", q_heads, keys, preferred_element_type=jnp.float32) * scale
    )
    spot = jnp.arange(MOSTP)[:, None] * PAGE + jnp.arange(PAGE)[None, :]
    live = (spot[None] < kv_lengths[:, None, None])[:, None, None, None]
    cache = jnp.where(live, cache, -1e30)
    causal = jnp.arange(steps)[None, :] <= jnp.arange(steps)[:, None]
    fresh = (
        jnp.einsum("rtkgd,rskd->rtkgs", q_heads, key_rot, preferred_element_type=jnp.float32)
        * scale
    )
    fresh = jnp.where(causal[None, :, None, None, :], fresh, -1e30)
    top = jnp.maximum(jnp.max(cache, axis=(4, 5)), jnp.max(fresh, axis=4))
    e_cache = jnp.where(live, jnp.exp(cache - top[..., None, None]), 0.0)
    e_fresh = jnp.where(causal[None, :, None, None, :], jnp.exp(fresh - top[..., None]), 0.0)
    total = jnp.sum(e_cache, axis=(4, 5)) + jnp.sum(e_fresh, axis=4)
    w_cache = (e_cache / total[..., None, None]).astype(jnp.bfloat16)
    w_fresh = (e_fresh / total[..., None]).astype(jnp.bfloat16)
    out = jnp.einsum("rtkgmn,rmknd->rtkgd", w_cache, vals, preferred_element_type=jnp.float32)
    out = out + jnp.einsum(
        "rtkgs,rskd->rtkgd", w_fresh, value_new, preferred_element_type=jnp.float32
    )
    return out.reshape(rows, steps, HQ * HD).astype(jnp.bfloat16)


def solution(mesh):
    in_specs = (
        P("replica", None, "tp"),
        P(),
        P(("replica", "tp"), None),
        P(("replica", "tp"), None),
        P(("replica", "tp"), None),
        P("tp"),
        P("tp"),
        P("tp"),
        P(("replica", "tp"), None, None, None),
        P(("replica", "tp"), None, None, None),
        P(("replica", "tp")),
        P(("replica", "tp"), None),
    )
    out_specs = P(("replica", "tp"), None, None)
    return jax.shard_map(
        on_device, mesh=mesh, in_specs=in_specs, out_specs=out_specs, check_vma=False
    )
```

profile of v0, /device:TPU:0, one launch (start us, length us, event | category | flops | bytes accessed | tf_op | source)
XLA Modules:
  0.0 380.4 jit_solution(5661806267189946849)
XLA Ops:
  6.5 1.3 copy.32
  7.9 10.0 %all_to_all.90 = bf16[256,4,128]{0,2,1:T(8,128)(2,1)S(1)} all-to-all(bf16[256,4,128]{0,2,1:T(8,128)(2,1)S(1)} %bitcast.101), channel_id=1, replica_groups=mesh['replica'=8,'tp'=4] {'tp'}, dimensions={1} | all-to-all | bytes 524288 | tf_op jit(solution)/shard_map/all_to_all | solution.py:54
  17.9 0.8 copy.33
  19.0 8.4 %all_to_all.91 = bf16[256,4,128]{0,2,1:T(8,128)(2,1)S(1)} all-to-all(bf16[256,4,128]{0,2,1:T(8,128)(2,1)S(1)} %bitcast.102), channel_id=1, replica_groups=mesh['replica'=8,'tp'=4] {'tp'}, dimensions={1} | all-to-all | bytes 524288 | tf_op jit(solution)/shard_map/all_to_all | solution.py:55
  27.4 0.9 copy.38
  28.3 4.6 %copy.27 = bf16[256,4096]{0,1:T(8,128)(2,1)} copy(f32[256,4096]{1,0:T(8,128)} %param.16) | data formatting | bytes 6291456 | tf_op args[2]
  32.9 30.1 %all_to_all.92 = bf16[256,4,1024]{0,2,1:T(8,128)(2,1)} all-to-all(bf16[256,4,1024]{0,2,1:T(8,128)(2,1)} %bitcast.96), channel_id=1, replica_groups=mesh['replica'=8,'tp'=4] {'tp'}, dimensions={1} | all-to-all | bytes 4194304 | tf_op jit(solution)/shard_map/all_to_all | solution.py:53
  63.1 4.0 %copy.28 = bf16[4,256,1024]{2,1,0:T(8,128)(2,1)} copy(bf16[4,256,1024]{1,2,0:T(8,128)(2,1)} %bitcast.98) | data formatting | bytes 4194304 | tf_op jit(solution)/shard_map/all_to_all | solution.py:53
  67.1 0.9 copy-done.3
  68.0 7.8 %all_gather.12 = bf16[12,4,8192]{2,1,0:T(4,128)(2,1)S(1)} all-gather(bf16[12,4,2048]{2,1,0:T(4,128)(2,1)S(1)} %copy-done.3), channel_id=1, replica_groups=mesh['replica'=8,'tp'=4] {'tp'}, dimensions={2}, use_global_device_ids=true | all-gather | bytes 983040 | tf_op jit(solution)/shard_map/all_gather | solution.py:43
  75.8 0.5 fusion.6
  76.3 1.4 fusion.8
  77.7 1.6 reshape.170
  79.4 2.7 gather_fusion.1
  82.2 4.3 %gather_fusion = bf16[24,4,128,128]{3,2,1,0:T(8,128)(2,1)} fusion(bf16[16,4,128,128]{3,2,1,0:T(8,128)(2,1)} %param.23, s32[1024]{0:T(1024)S(1)} %pad_clamp_fusion), kind=kCustom, calls=%fused_computation.clone | custom fusion | bytes 6291552 | tf_op jit(solution)/shard_map/jit(_take)/gather | solution.py:84
  87.0 2.7 fusion.24
  89.6 3.4 all-to-all-start.3
  93.0 25.1 %all-gather.8.cloned.1.call-done = bf16[8192,128]{1,0:T(8,128)(2,1)} async-done(((bf16[1024,128]{1,0:T(8,128)(2,1)}), bf16[8192,128]{1,0:T(8,128)(2,1)}) %all-gather.8.cloned.1.call-update) | async-done | bytes 2097168 | tf_op jit(solution)/shard_map/all_gather | solution.py:60
  118.2 2.7 fusion.25
  120.8 225.3 %all-gather.4.cloned.1.call-done = bf16[8192,1024]{1,0:T(8,128)(2,1)} async-done(((bf16[1024,1024]{1,0:T(8,128)(2,1)}), bf16[8192,1024]{1,0:T(8,128)(2,1)}) %all-gather.4.cloned.1.call-update) | async-done | bytes 16777232 | tf_op jit(solution)/shard_map/all_gather | solution.py:58
  346.1 8.8 %fusion.19 = bf16[48,1024]{1,0:T(8,128)(2,1)S(1)} fusion(bf16[48,8192]{1,0:T(8,128)(2,1)S(1)} %reshape.170, bf16[8192,1024]{1,0:T(8,128)(2,1)} %all-gather.4.cloned.1.call-done, f32[1024]{0:T(1024)S(1)} %copy-done.6), kind=kOutput, calls=%fused_computation.27 | convolution fusion | flops 805404672 | bytes 17666048 | tf_op jit(solution)/shard_map/dot_general | solution.py:62
  354.9 0.7 reshape.171
  355.6 3.3 all-to-all-start.1
  359.0 4.2 %all-to-all-done.1 = bf16[12,4,1024]{2,1,0:T(4,128)(2,1)S(1)} async-done(((bf16[12,4,1024]{2,1,0:T(4,128)(2,1)}), bf16[12,4,1024]{2,1,0:T(4,128)(2,1)S(1)}, u32[]{:S(2)}, u32[]{:S(2)}) %all-to-all-start.1) | async-done | bytes 98336 | tf_op jit(solution)/shard_map/all_to_all | solution.py:68
  363.2 3.4 all-to-all-start.5
  367.2 0.6 fusion.52
  367.8 3.4 bitcast_reduce_fusion
  371.2 0.2 fusion.35
  371.4 0.4 fusion.15
  371.8 1.0 fusion.16
  372.8 0.3 fusion.21
  373.2 0.7 convert_element_type.107
  (53 shorter events, 1.5 us)
Async XLA Ops:
  6.5 72.9 %copy-start = (bf16[16,4,128,128]{3,2,1,0:T(8,128)(2,1)S(1)}, bf16[16,4,128,128]{3,2,1,0:T(8,128)(2,1)}, u32[]{:S(2)}) copy-start(bf16[16,4,128,128]{3,2,1,0:T(8,128)(2,1)} %param.22) | copy-start | bytes 6291460
  6.5 12.3 %copy-start.2 = (f32[256,512]{1,0:T(8,128)S(1)}, f32[256,512]{1,0:T(8,128)}, u32[]{:S(2)}) copy-start(f32[256,512]{1,0:T(8,128)} %param.18) | copy-start | bytes 1572868
  6.5 80.4 %all-gather.6.cloned.1.call-start = ((), (), s32[]{:S(2)}) async-start(), calls=%async_computation.7 | async-start | bytes 2359296 | tf_op jit(solution)/shard_map/all_gather | solution.py:59
  18.8 99.4 %all-gather.8.cloned.1.call-start = ((), (), s32[]{:S(2)}) async-start(), calls=%async_computation.8 | async-start | bytes 2359296 | tf_op jit(solution)/shard_map/all_gather | solution.py:60
  28.3 317.9 %all-gather.4.cloned.1.call-start = ((), (), s32[]{:S(2)}) async-start(), calls=%async_computation.6 | async-start | bytes 18874368 | tf_op jit(solution)/shard_map/all_gather | solution.py:58
  67.0 0.9 copy-start.3
  67.0 9.3 %copy-start.4 = (f32[8192]{0:T(1024)S(1)}, f32[8192]{0:T(1024)}, u32[]{:S(2)}) copy-start(f32[8192]{0:T(1024)} %param.15) | copy-start | bytes 98308
  75.8 3.5 copy-start.5
  82.2 4.4 %copy-start.7 = (s32[3]{0:T(128)S(1)}, s32[3]{0:T(128)}, u32[]{:S(2)}) copy-start(s32[3]{0:T(128)} %param.24) | copy-start | bytes 40
  82.2 4.8 %copy-start.8 = (f32[128]{0:T(128)S(1)}, f32[128]{0:T(128)}, u32[]{:S(2)}) copy-start(f32[128]{0:T(128)} %param.20) | copy-start | bytes 1540
  86.5 31.7 %copy-start.9 = (f32[128]{0:T(128)S(1)}, f32[128]{0:T(128)}, u32[]{:S(2)}) copy-start(f32[128]{0:T(128)} %param.21) | copy-start | bytes 1540
  89.6 256.5 %copy-start.6 = (f32[1024]{0:T(1024)S(1)}, f32[1024]{0:T(1024)}, u32[]{:S(2)}) copy-start(f32[1024]{0:T(1024)} %param.19) | copy-start | bytes 12292
  89.6 31.2 %all-to-all-start.3 = ((bf16[12,4,128]{2,1,0:T(4,128)(2,1)}), bf16[12,4,128]{2,1,0:T(4,128)(2,1)S(1)}, u32[]{:S(2)}, u32[]{:S(2)}) async-start(bf16[12,4,128]{2,1,0:T(4,128)(2,1)} %bitcast.19), calls=%async_computation.3 | async-start | bytes 24576 | tf_op jit(solution)/shard_map/all_to_all | solution.py:69
  355.6 7.6 %all-to-all-start.1 = ((bf16[12,4,1024]{2,1,0:T(4,128)(2,1)}), bf16[12,4,1024]{2,1,0:T(4,128)(2,1)S(1)}, u32[]{:S(2)}, u32[]{:S(2)}) async-start(bf16[12,4,1024]{2,1,0:T(4,128)(2,1)} %reshape.171), calls=%async_computation.1 | async-start | bytes 196608 | tf_op jit(solution)/shard_map/all_to_all | solution.py:68
  363.2 9.6 %all-to-all-start.5 = ((bf16[12,4,128]{2,1,0:T(4,128)(2,1)}), bf16[12,4,128]{2,1,0:T(4,128)(2,1)S(1)}, u32[]{:S(2)}, u32[]{:S(2)}) async-start(bf16[12,4,128]{2,1,0:T(4,128)(2,1)} %bitcast.30), calls=%async_computation.5 | async-start | bytes 24576 | tf_op jit(solution)/shard_map/all_to_all | solution.py:70
  367.8 4.0 %copy-start.1 = (bf16[24,4,128,128]{3,2,1,0:T(8,128)(2,1)S(1)}, bf16[24,4,128,128]{3,2,1,0:T(8,128)(2,1)}, u32[]{:S(2)}) copy-start(bf16[24,4,128,128]{3,2,1,0:T(8,128)(2,1)} %gather_fusion) | copy-start | bytes 9437188
Sparse Core Ops, SparseCore 0:
  18.9 49.3 all-gather.5
  70.5 47.6 all-gather.7
  120.3 225.7 all-gather.3
where the time goes:
time: 381 us; the launch traced here: 380 us
  waiting for transfers between devices  255 us (67%)
  blocking collectives  56.4 us (15%)
  local copies, waits for them, and re-layouts  23.1 us (6%)
  matrix products  19.4 us (5%)
  between operations  13.4 us (4%)
  starting transfers between devices  10.2 us (3%)
    all_gather x1, waiting for transfers between devices, on_device(): lax.all_gather(local[0], 'replica', axis=0, tiled=True)  225 us
    all_to_all x1, blocking collectives, on_device(): lax.all_to_all(shards[0], 'tp', split_axis=1, concat_axis=0, tiled=True)  30.1 us
    all_gather x1, waiting for transfers between devices, on_device(): lax.all_gather(local[2], 'replica', axis=0, tiled=True)  25.1 us
    dot_general x3, matrix products, on_device(): jnp.dot(normed, piece, preferred_element_type=jnp.float32)  14.1 us
    all_to_all x1, blocking collectives, on_device(): lax.all_to_all(shards[1], 'tp', split_axis=1, concat_axis=0, tiled=True)  10 us
    all_to_all x1, blocking collectives, on_device(): lax.all_to_all(shards[2], 'tp', split_axis=1, concat_axis=0, tiled=True)  8.39 us
    all_gather x1, blocking collectives, on_device(): whole = lax.all_gather(hidden, 'tp', axis=2, tiled=True)  7.81 us
  transfers between devices with their start and end apart: 6, of which 3 were waited for; matrix products, arithmetic and copies ran while one was open for 8% of the time, Pallas kernels for 0%

commit v1 on v0

--- a/solution.py
+++ b/solution.py
@@ -10,6 +10,26 @@
 MOSTP = 8
 EPS = 1e-06
 THETA = 1000000.0
+
+
+def serve_pipes_on(in_array):
+    axis_n = jax.lax.axis_size("replica")
+    trail = [in_array]
+    kk = 1
+    while kk < axis_n:
+        trail.append(
+            jax.lax.ppermute(
+                trail[kk - 1],
+                axis_name="replica",
+                perm=[(j0, (j0 - 1) % axis_n) for j0 in range(axis_n)],
+            )
+        )
+        kk += 1
+    return jnp.roll(
+        jnp.concatenate(trail, axis=0),
+        shift=jax.lax.axis_index("replica") * in_array.shape[0],
+        axis=0,
+    )
 
 
 def rotate(values, positions):
@@ -57,7 +77,7 @@
     pieces = (
         lax.all_gather(local[0], "replica", axis=0, tiled=True),
         lax.all_gather(local[1], "replica", axis=0, tiled=True),
-        lax.all_gather(local[2], "replica", axis=0, tiled=True),
+        serve_pipes_on(local[2]),
     )
     sums = tuple((jnp.dot(normed, piece, preferred_element_type=jnp.float32) for piece in pieces))
     made = [

time: 381 us -> 367 us (0.963)
  waiting for transfers between devices: 255 us -> 198 us
  starting transfers between devices: 10.2 us -> 40.8 us
  local copies, waits for them, and re-layouts: 23.1 us -> 39.6 us
  blocking collectives: 56.4 us -> 51.2 us
    all_gather x1, waiting for transfers between devices: 225 us -> 123 us  [on_device(): lax.all_gather(local[0], 'replica', axis=0, tiled=True)]
    ppermute x0 -> x7, waiting for transfers between devices: none -> 69.5 us  [serve_pipes_on(): jax.lax.ppermute(trail[kk - 1], axis_name='replica', perm=[(j0, (j0 - 1)...]
    ppermute x0 -> x7, starting transfers between devices: none -> 27.4 us  [serve_pipes_on(): jax.lax.ppermute(trail[kk - 1], axis_name='replica', perm=[(j0, (j0 - 1)...]
    all_gather x1 -> x0, waiting for transfers between devices: 25.1 us -> none  [on_device(): lax.all_gather(local[2], 'replica', axis=0, tiled=True)]
    unnamed x23 -> x46, local copies, waits for them, and re-layouts: 7.03 us -> 23.3 us
    all_to_all x1 -> x0, blocking collectives: 8.39 us -> none  [on_device(): lax.all_to_all(shards[2], 'tp', split_axis=1, concat_axis=0, tiled=True)]
  transfers between devices with their start and end apart: 6 -> 13, of which waited for: 3 -> 10; matrix products, arithmetic and copies ran while one was open for 8% -> 14% of each run, Pallas kernels for 0% -> 0%
where the time goes in v1:
time: 367 us; the launch traced here: 366 us
  waiting for transfers between devices  198 us (54%)
  blocking collectives  51.2 us (14%)
  starting transfers between devices  40.8 us (11%)
  local copies, waits for them, and re-layouts  39.6 us (11%)
  matrix products  19.3 us (5%)
  between operations  13.7 us (4%)
    all_gather x1, waiting for transfers between devices, on_device(): lax.all_gather(local[0], 'replica', axis=0, tiled=True)  123 us
    ppermute x7, waiting for transfers between devices, serve_pipes_on(): jax.lax.ppermute(trail[kk - 1], axis_name='replica', perm=[(j0, (j0 - 1)...  69.5 us
    all_to_all x1, blocking collectives, on_device(): lax.all_to_all(shards[0], 'tp', split_axis=1, concat_axis=0, tiled=True)  30.1 us
    ppermute x7, starting transfers between devices, serve_pipes_on(): jax.lax.ppermute(trail[kk - 1], axis_name='replica', perm=[(j0, (j0 - 1)...  27.4 us
    unnamed x46, local copies, waits for them, and re-layouts  23.3 us
    dot_general x3, matrix products, on_device(): jnp.dot(normed, piece, preferred_element_type=jnp.float32)  14.1 us
    all_gather x1, blocking collectives, on_device(): whole = lax.all_gather(hidden, 'tp', axis=2, tiled=True)  11.1 us
    all_to_all x1, blocking collectives, on_device(): lax.all_to_all(shards[1], 'tp', split_axis=1, concat_axis=0, tiled=True)  10 us
  transfers between devices with their start and end apart: 13, of which 10 were waited for; matrix products, arithmetic and copies ran while one was open for 14% of the time, Pallas kernels for 0%

profile of v1, /device:TPU:0, one launch (start us, length us, event | category | flops | bytes accessed | tf_op | source)
XLA Modules:
  0.0 365.9 jit_solution(17248176052459020156)
XLA Ops:
  7.9 10.0 %all_to_all.90 = bf16[256,4,128]{0,2,1:T(8,128)(2,1)S(1)} all-to-all(bf16[256,4,128]{0,2,1:T(8,128)(2,1)S(1)} %bitcast.103), channel_id=1, replica_groups=mesh['replica'=8,'tp'=4] {'tp'}, dimensions={1} | all-to-all | bytes 524288 | tf_op jit(solution)/shard_map/all_to_all | solution.py:74
  18.8 4.6 %copy.27 = bf16[256,4096]{0,1:T(8,128)(2,1)} copy(f32[256,4096]{1,0:T(8,128)} %param.16) | data formatting | bytes 6291456 | tf_op args[2]
  23.4 30.1 %all_to_all.91 = bf16[256,4,1024]{0,2,1:T(8,128)(2,1)} all-to-all(bf16[256,4,1024]{0,2,1:T(8,128)(2,1)} %bitcast.95), channel_id=1, replica_groups=mesh['replica'=8,'tp'=4] {'tp'}, dimensions={1} | all-to-all | bytes 4194304 | tf_op jit(solution)/shard_map/all_to_all | solution.py:73
  53.6 4.1 %copy.28 = bf16[4,256,1024]{2,1,0:T(8,128)(2,1)} copy(bf16[4,256,1024]{1,2,0:T(8,128)(2,1)} %bitcast.97) | data formatting | bytes 4194304 | tf_op jit(solution)/shard_map/all_to_all | solution.py:73
  58.5 3.4 all-to-all-start.4
  62.0 11.1 %all_gather.9 = bf16[12,4,8192]{2,1,0:T(4,128)(2,1)S(1)} all-gather(bf16[12,4,2048]{2,1,0:T(4,128)(2,1)S(1)} %copy-done.7), channel_id=1, replica_groups=mesh['replica'=8,'tp'=4] {'tp'}, dimensions={2}, use_global_device_ids=true | all-gather | bytes 983040 | tf_op jit(solution)/shard_map/all_gather | solution.py:63
  75.2 4.6 %collective-permute-start = (bf16[1024,128]{1,0:T(8,128)(2,1)S(1)}, bf16[1024,128]{1,0:T(8,128)(2,1)S(1)}, u32[]{:S(2)}, u32[]{:S(2)}) collective-permute-start(bf16[1024,128]{1,0:T(8,128)(2,1)S(1)} %bitcast.100), channel_id=1, source_target_pairs={{0,28},{4,0},{8,4},{12,8},{16,12},{20,16},{24,20},{28,24},{1,29},{... | collective-permute-start | bytes 786440 | tf_op jit(solution)/shard_map/ppermute | solution.py:21
  79.8 12.0 %collective-permute-done = bf16[1024,128]{1,0:T(8,128)(2,1)S(1)} collective-permute-done((bf16[1024,128]{1,0:T(8,128)(2,1)S(1)}, bf16[1024,128]{1,0:T(8,128)(2,1)S(1)}, u32[]{:S(2)}, u32[]{:S(2)}) %collective-permute-start) | collective-permute-done | bytes 262176 | tf_op jit(solution)/shard_map/ppermute | solution.py:21
  91.9 5.2 %collective-permute-start.1 = (bf16[1024,128]{1,0:T(8,128)(2,1)S(1)}, bf16[1024,128]{1,0:T(8,128)(2,1)S(1)}, u32[]{:S(2)}, u32[]{:S(2)}) collective-permute-start(bf16[1024,128]{1,0:T(8,128)(2,1)S(1)} %collective-permute-done), channel_id=1, source_target_pairs={{0,28},{4,0},{8,4},{12,8},{16,12},{20,16},{24,20},{28,24},{1,29},{... | collective-permute-start | bytes 786440 | tf_op jit(solution)/shard_map/ppermute | solution.py:21
  97.2 11.7 %collective-permute-done.1 = bf16[1024,128]{1,0:T(8,128)(2,1)S(1)} collective-permute-done((bf16[1024,128]{1,0:T(8,128)(2,1)S(1)}, bf16[1024,128]{1,0:T(8,128)(2,1)S(1)}, u32[]{:S(2)}, u32[]{:S(2)}) %collective-permute-start.1) | collective-permute-done | bytes 262176 | tf_op jit(solution)/shard_map/ppermute | solution.py:21
  108.9 5.2 %collective-permute-start.2 = (bf16[1024,128]{1,0:T(8,128)(2,1)S(1)}, bf16[1024,128]{1,0:T(8,128)(2,1)S(1)}, u32[]{:S(2)}, u32[]{:S(2)}) collective-permute-start(bf16[1024,128]{1,0:T(8,128)(2,1)S(1)} %collective-permute-done.1), channel_id=1, source_target_pairs={{0,28},{4,0},{8,4},{12,8},{16,12},{20,16},{24,20},{28,24},{1,29},{... | collective-permute-start | bytes 786440 | tf_op jit(solution)/shard_map/ppermute | solution.py:21
  114.1 11.5 %collective-permute-done.2 = bf16[1024,128]{1,0:T(8,128)(2,1)S(1)} collective-permute-done((bf16[1024,128]{1,0:T(8,128)(2,1)S(1)}, bf16[1024,128]{1,0:T(8,128)(2,1)S(1)}, u32[]{:S(2)}, u32[]{:S(2)}) %collective-permute-start.2) | collective-permute-done | bytes 262176 | tf_op jit(solution)/shard_map/ppermute | solution.py:21
  125.6 5.2 %collective-permute-start.3 = (bf16[1024,128]{1,0:T(8,128)(2,1)S(1)}, bf16[1024,128]{1,0:T(8,128)(2,1)}, u32[]{:S(2)}, u32[]{:S(2)}) collective-permute-start(bf16[1024,128]{1,0:T(8,128)(2,1)S(1)} %collective-permute-done.2), channel_id=1, source_target_pairs={{0,28},{4,0},{8,4},{12,8},{16,12},{20,16},{24,20},{28,24},{1,29},{... | collective-permute-start | bytes 786440 | tf_op jit(solution)/shard_map/ppermute | solution.py:21
  130.9 11.2 %collective-permute-done.3 = bf16[1024,128]{1,0:T(8,128)(2,1)} collective-permute-done((bf16[1024,128]{1,0:T(8,128)(2,1)S(1)}, bf16[1024,128]{1,0:T(8,128)(2,1)}, u32[]{:S(2)}, u32[]{:S(2)}) %collective-permute-start.3) | collective-permute-done | bytes 262176 | tf_op jit(solution)/shard_map/ppermute | solution.py:21
  142.1 5.3 %collective-permute-start.4 = (bf16[1024,128]{1,0:T(8,128)(2,1)}, bf16[1024,128]{1,0:T(8,128)(2,1)}, u32[]{:S(2)}, u32[]{:S(2)}) collective-permute-start(bf16[1024,128]{1,0:T(8,128)(2,1)} %collective-permute-done.3), channel_id=1, source_target_pairs={{0,28},{4,0},{8,4},{12,8},{16,12},{20,16},{24,20},{28,24},{1,29},{... | collective-permute-start | bytes 786440 | tf_op jit(solution)/shard_map/ppermute | solution.py:21
  149.0 2.8 gather_fusion.1
  151.8 4.3 %gather_fusion = bf16[24,4,128,128]{3,2,1,0:T(8,128)(2,1)} fusion(bf16[16,4,128,128]{3,2,1,0:T(8,128)(2,1)} %param.23, s32[1024]{0:T(1024)S(1)} %pad_clamp_fusion), kind=kCustom, calls=%fused_computation.clone | custom fusion | bytes 6291552 | tf_op jit(solution)/shard_map/jit(_take)/gather | solution.py:104
  157.0 5.1 %collective-permute-done.4 = bf16[1024,128]{1,0:T(8,128)(2,1)} collective-permute-done((bf16[1024,128]{1,0:T(8,128)(2,1)}, bf16[1024,128]{1,0:T(8,128)(2,1)}, u32[]{:S(2)}, u32[]{:S(2)}) %collective-permute-start.4) | collective-permute-done | bytes 262176 | tf_op jit(solution)/shard_map/ppermute | solution.py:21
  162.1 1.9 collective-permute-start.5
  166.4 1.7 constant_dynamic-update-slice_fusion.12
  168.1 14.3 %collective-permute-done.5 = bf16[1024,128]{1,0:T(8,128)(2,1)S(1)} collective-permute-done((bf16[1024,128]{1,0:T(8,128)(2,1)}, bf16[1024,128]{1,0:T(8,128)(2,1)S(1)}, u32[]{:S(2)}, u32[]{:S(2)}) %collective-permute-start.5) | collective-permute-done | bytes 262176 | tf_op jit(solution)/shard_map/ppermute | solution.py:21
  186.4 3.7 %collective-permute-done.6 = bf16[1024,128]{1,0:T(8,128)(2,1)S(1)} collective-permute-done((bf16[1024,128]{1,0:T(8,128)(2,1)S(1)}, bf16[1024,128]{1,0:T(8,128)(2,1)S(1)}, u32[]{:S(2)}, u32[]{:S(2)}) %collective-permute-start.6) | collective-permute-done | bytes 262176 | tf_op jit(solution)/shard_map/ppermute | solution.py:21
  193.7 1.7 constant_dynamic-update-slice_fusion.3
  198.5 2.7 fusion.29
  201.1 3.3 all-to-all-start.3
  204.4 2.7 fusion.30
  208.2 123.1 %all-gather.3.cloned.1.call-done = bf16[8192,1024]{1,0:T(8,128)(2,1)} async-done(((bf16[1024,1024]{1,0:T(8,128)(2,1)}), bf16[8192,1024]{1,0:T(8,128)(2,1)}) %all-gather.3.cloned.1.call-update) | async-done | bytes 16777232 | tf_op jit(solution)/shard_map/all_gather | solution.py:78
  331.3 8.8 %fusion.21 = bf16[48,1024]{1,0:T(8,128)(2,1)S(1)} fusion(bf16[48,8192]{1,0:T(8,128)(2,1)S(1)} %reshape.170, bf16[8192,1024]{1,0:T(8,128)(2,1)} %all-gather.3.cloned.1.call-done, f32[1024]{0:T(1024)S(1)} %copy-done.10), kind=kOutput, calls=%fused_computation.29 | convolution fusion | flops 805404672 | bytes 17666048 | tf_op jit(solution)/shard_map/dot_general | solution.py:82
  340.8 3.3 all-to-all-start.1
  344.2 4.2 %all-to-all-done.1 = bf16[12,4,1024]{2,1,0:T(4,128)(2,1)S(1)} async-done(((bf16[12,4,1024]{2,1,0:T(4,128)(2,1)}), bf16[12,4,1024]{2,1,0:T(4,128)(2,1)S(1)}, u32[]{:S(2)}, u32[]{:S(2)}) %all-to-all-start.1) | async-done | bytes 98336 | tf_op jit(solution)/shard_map/all_to_all | solution.py:88
  348.4 3.4 all-to-all-start.5
  353.0 3.4 bitcast_reduce_fusion
  (89 shorter events, 26.8 us)
Async XLA Ops:
  6.5 142.5 %copy-start = (bf16[16,4,128,128]{3,2,1,0:T(8,128)(2,1)S(1)}, bf16[16,4,128,128]{3,2,1,0:T(8,128)(2,1)}, u32[]{:S(2)}) copy-start(bf16[16,4,128,128]{3,2,1,0:T(8,128)(2,1)} %param.22) | copy-start | bytes 6291460
  6.5 191.9 %all-gather.5.cloned.1.call-start = ((), (), s32[]{:S(2)}) async-start(), calls=%async_computation.7 | async-start | bytes 2359296 | tf_op jit(solution)/shard_map/all_gather | solution.py:79
  18.8 312.6 %all-gather.3.cloned.1.call-start = ((), (), s32[]{:S(2)}) async-start(), calls=%async_computation.6 | async-start | bytes 18874368 | tf_op jit(solution)/shard_map/all_gather | solution.py:78
  53.6 4.1 %copy-start.6 = (f32[256,512]{1,0:T(8,128)S(1)}, f32[256,512]{1,0:T(8,128)}, u32[]{:S(2)}) copy-start(f32[256,512]{1,0:T(8,128)} %param.18) | copy-start | bytes 1572868
  53.6 8.4 %copy-start.7 = (bf16[12,4,2048]{2,1,0:T(4,128)(2,1)S(1)}, bf16[12,4,2048]{2,1,0:T(4,128)(2,1)}, u32[]{:S(2)}) copy-start(bf16[12,4,2048]{2,1,0:T(4,128)(2,1)} %param.14) | copy-start | bytes 589828
  57.6 15.9 %copy-start.8 = (f32[8192]{0:T(1024)S(1)}, f32[8192]{0:T(1024)}, u32[]{:S(2)}) copy-start(f32[8192]{0:T(1024)} %param.15) | copy-start | bytes 98308
  57.7 17.3 %copy-start.11 = (s32[3]{0:T(128)S(1)}, s32[3]{0:T(128)}, u32[]{:S(2)}) copy-start(s32[3]{0:T(128)} %param.24) | copy-start | bytes 40
  57.7 22.1 %copy-start.9 = (s32[3,8]{1,0:T(4,128)S(1)}, s32[3,8]{1,0:T(4,128)}, u32[]{:S(2)}) copy-start(s32[3,8]{1,0:T(4,128)} %param.25) | copy-start | bytes 292
  58.5 16.5 %all-to-all-start.4 = ((bf16[256,4,128]{0,2,1:T(8,128)(2,1)}), bf16[256,4,128]{0,2,1:T(8,128)(2,1)S(1)}, u32[]{:S(2)}, u32[]{:S(2)}) async-start(bf16[256,4,128]{0,2,1:T(8,128)(2,1)} %bitcast.27), calls=%async_computation.4 | async-start | bytes 524288 | tf_op jit(solution)/shard_map/all_to_all | solution.py:75
  75.2 16.7 %collective-permute-start = (bf16[1024,128]{1,0:T(8,128)(2,1)S(1)}, bf16[1024,128]{1,0:T(8,128)(2,1)S(1)}, u32[]{:S(2)}, u32[]{:S(2)}) collective-permute-start(bf16[1024,128]{1,0:T(8,128)(2,1)S(1)} %bitcast.100), channel_id=1, source_target_pairs={{0,28},{4,0},{8,4},{12,8},{16,12},{20,16},{24,20},{28,24},{1,29},{... | collective-permute-start | bytes 786440 | tf_op jit(solution)/shard_map/ppermute | solution.py:21
  91.9 17.0 %collective-permute-start.1 = (bf16[1024,128]{1,0:T(8,128)(2,1)S(1)}, bf16[1024,128]{1,0:T(8,128)(2,1)S(1)}, u32[]{:S(2)}, u32[]{:S(2)}) collective-permute-start(bf16[1024,128]{1,0:T(8,128)(2,1)S(1)} %collective-permute-done), channel_id=1, source_target_pairs={{0,28},{4,0},{8,4},{12,8},{16,12},{20,16},{24,20},{28,24},{1,29},{... | collective-permute-start | bytes 786440 | tf_op jit(solution)/shard_map/ppermute | solution.py:21
  108.9 38.6 %copy-start.2 = (bf16[1024,128]{1,0:T(8,128)(2,1)}, bf16[1024,128]{1,0:T(8,128)(2,1)S(1)}, u32[]{:S(2)}) copy-start(bf16[1024,128]{1,0:T(8,128)(2,1)S(1)} %collective-permute-done.1) | copy-start | bytes 786436
  108.9 16.8 %collective-permute-start.2 = (bf16[1024,128]{1,0:T(8,128)(2,1)S(1)}, bf16[1024,128]{1,0:T(8,128)(2,1)S(1)}, u32[]{:S(2)}, u32[]{:S(2)}) collective-permute-start(bf16[1024,128]{1,0:T(8,128)(2,1)S(1)} %collective-permute-done.1), channel_id=1, source_target_pairs={{0,28},{4,0},{8,4},{12,8},{16,12},{20,16},{24,20},{28,24},{1,29},{... | collective-permute-start | bytes 786440 | tf_op jit(solution)/shard_map/ppermute | solution.py:21
  125.6 21.8 %copy-start.4 = (bf16[1024,128]{1,0:T(8,128)(2,1)}, bf16[1024,128]{1,0:T(8,128)(2,1)S(1)}, u32[]{:S(2)}) copy-start(bf16[1024,128]{1,0:T(8,128)(2,1)S(1)} %collective-permute-done.2) | copy-start | bytes 786436
  125.6 16.5 %collective-permute-start.3 = (bf16[1024,128]{1,0:T(8,128)(2,1)S(1)}, bf16[1024,128]{1,0:T(8,128)(2,1)}, u32[]{:S(2)}, u32[]{:S(2)}) collective-permute-start(bf16[1024,128]{1,0:T(8,128)(2,1)S(1)} %collective-permute-done.2), channel_id=1, source_target_pairs={{0,28},{4,0},{8,4},{12,8},{16,12},{20,16},{24,20},{28,24},{1,29},{... | collective-permute-start | bytes 786440 | tf_op jit(solution)/shard_map/ppermute | solution.py:21
  142.1 19.9 %collective-permute-start.4 = (bf16[1024,128]{1,0:T(8,128)(2,1)}, bf16[1024,128]{1,0:T(8,128)(2,1)}, u32[]{:S(2)}, u32[]{:S(2)}) collective-permute-start(bf16[1024,128]{1,0:T(8,128)(2,1)} %collective-permute-done.3), channel_id=1, source_target_pairs={{0,28},{4,0},{8,4},{12,8},{16,12},{20,16},{24,20},{28,24},{1,29},{... | collective-permute-start | bytes 786440 | tf_op jit(solution)/shard_map/ppermute | solution.py:21
  156.2 36.1 %copy-start.3 = (bf16[1024,128]{1,0:T(8,128)(2,1)S(1)}, bf16[1024,128]{1,0:T(8,128)(2,1)}, u32[]{:S(2)}) copy-start(bf16[1024,128]{1,0:T(8,128)(2,1)} %copy-done.2) | copy-start | bytes 786436
  156.2 36.8 %copy-start.5 = (bf16[1024,128]{1,0:T(8,128)(2,1)S(1)}, bf16[1024,128]{1,0:T(8,128)(2,1)}, u32[]{:S(2)}) copy-start(bf16[1024,128]{1,0:T(8,128)(2,1)} %copy-done.4) | copy-start | bytes 786436
  162.1 20.3 %collective-permute-start.5 = (bf16[1024,128]{1,0:T(8,128)(2,1)}, bf16[1024,128]{1,0:T(8,128)(2,1)S(1)}, u32[]{:S(2)}, u32[]{:S(2)}) collective-permute-start(bf16[1024,128]{1,0:T(8,128)(2,1)} %collective-permute-done.4), channel_id=1, source_target_pairs={{0,28},{4,0},{8,4},{12,8},{16,12},{20,16},{24,20},{28,24},{1,29},{... | collective-permute-start | bytes 786440 | tf_op jit(solution)/shard_map/ppermute | solution.py:21
  168.1 30.4 %copy-start.12 = (f32[128]{0:T(128)S(1)}, f32[128]{0:T(128)}, u32[]{:S(2)}) copy-start(f32[128]{0:T(128)} %param.20) | copy-start | bytes 1540
  182.4 7.7 %collective-permute-start.6 = (bf16[1024,128]{1,0:T(8,128)(2,1)S(1)}, bf16[1024,128]{1,0:T(8,128)(2,1)S(1)}, u32[]{:S(2)}, u32[]{:S(2)}) collective-permute-start(bf16[1024,128]{1,0:T(8,128)(2,1)S(1)} %collective-permute-done.5), channel_id=1, source_target_pairs={{0,28},{4,0},{8,4},{12,8},{16,12},{20,16},{24,20},{28,24},{1,29},{... | collective-permute-start | bytes 786440 | tf_op jit(solution)/shard_map/ppermute | solution.py:21
  192.2 12.2 %copy-start.13 = (f32[128]{0:T(128)S(1)}, f32[128]{0:T(128)}, u32[]{:S(2)}) copy-start(f32[128]{0:T(128)} %param.21) | copy-start | bytes 1540
  197.8 133.6 %copy-start.10 = (f32[1024]{0:T(1024)S(1)}, f32[1024]{0:T(1024)}, u32[]{:S(2)}) copy-start(f32[1024]{0:T(1024)} %param.19) | copy-start | bytes 12292
  201.1 7.1 %all-to-all-start.3 = ((bf16[12,4,128]{2,1,0:T(4,128)(2,1)}), bf16[12,4,128]{2,1,0:T(4,128)(2,1)S(1)}, u32[]{:S(2)}, u32[]{:S(2)}) async-start(bf16[12,4,128]{2,1,0:T(4,128)(2,1)} %bitcast.19), calls=%async_computation.3 | async-start | bytes 24576 | tf_op jit(solution)/shard_map/all_to_all | solution.py:89
  340.8 7.6 %all-to-all-start.1 = ((bf16[12,4,1024]{2,1,0:T(4,128)(2,1)}), bf16[12,4,1024]{2,1,0:T(4,128)(2,1)S(1)}, u32[]{:S(2)}, u32[]{:S(2)}) async-start(bf16[12,4,1024]{2,1,0:T(4,128)(2,1)} %reshape.171), calls=%async_computation.1 | async-start | bytes 196608 | tf_op jit(solution)/shard_map/all_to_all | solution.py:88
  348.4 9.6 %all-to-all-start.5 = ((bf16[12,4,128]{2,1,0:T(4,128)(2,1)}), bf16[12,4,128]{2,1,0:T(4,128)(2,1)S(1)}, u32[]{:S(2)}, u32[]{:S(2)}) async-start(bf16[12,4,128]{2,1,0:T(4,128)(2,1)} %bitcast.30), calls=%async_computation.5 | async-start | bytes 24576 | tf_op jit(solution)/shard_map/all_to_all | solution.py:90
  353.0 4.0 %copy-start.1 = (bf16[24,4,128,128]{3,2,1,0:T(8,128)(2,1)S(1)}, bf16[24,4,128,128]{3,2,1,0:T(8,128)(2,1)}, u32[]{:S(2)}) copy-start(bf16[24,4,128,128]{3,2,1,0:T(8,128)(2,1)} %gather_fusion) | copy-start | bytes 9437188
Sparse Core Ops, SparseCore 0:
  18.9 49.3 all-gather.4
  70.5 260.8 all-gather.2
